TPU v7x, 32 devices: a whole 2x2x4 slice. The times are simulated.
32 devices in a mesh: station: 4 (over z), group: 4 (over x, core), bias: 2 (over y).
Axes of the slice: x: 2, y: 2, z: 4, core: 2. Of those that a mesh axis runs over, the one named last changes fastest.
Arguments:
- normal_mat: float32 [128, 2304], P(('station', 'group')), may hold values from -16 to 18, as said below
- coupling: float32 [128, 2, 8, 48, 128], P(('station', 'group'), 'bias'), may hold values from -0.13258252 to 0.13258252
- lengths: int32 [128], P(('station', 'group')), may hold values from 12 to 48
- visible: int32 [128, 2, 8], P(('station', 'group'), 'bias'), may hold values from 0 to 16, as said below
- bias_prior: float32 [2, 16, 128], P('bias', 'station'), may hold values from 0.1 to 1
- unimod: int32 [128, 2304], P(('station', 'group')), may hold values from -1 to 2, as said below
Outputs:
- bias_cov: float32 [2, 16, 128, 128], P('bias', 'station')
- amb_cov: float32 [128, 2304], P(('station', 'group'))
Inputs may be any that keep to these rules, and one draw needn't show every extreme that they name: `normal_mat`: each station's matrix, read as 48 x 48 row by row, is symmetric with all eigenvalues 1 or more. Each list visible[s, h] holds distinct block numbers below 16 in its first slots and the value 16 in its unused slots; every list has at least one block; in every draw the stations of some devices use all 8 slots. `unimod`: each station's matrix, read as 48 x 48 row by row, is a unit lower triangular times a unit upper triangular integer matrix; each row of the lower factor and each column of the upper factor holds at most one entry off the diagonal, -1 or 1; so every leading square block has determinant 1.
All inputs are finite; a program needn't handle non-finite values.
Results may differ from a plain program's by a relative error of at most 0.0003.
Values sent between devices are 32-bit elements; how exact they have to be, the bound alone decides.
No kernel may reach another device: no remote copies, remote signals or barrier semaphores. Data moves between devices by JAX's collectives and lax.ppermute only.
A program may use at most 64 MiB of HBM per device.

v0:
```python
import jax
import jax.numpy as jnp
from jax import lax
from jax.sharding import PartitionSpec as P

NHALF = 16
precise = lax.Precision.HIGHEST


def spd_inverse(matrix):
    matrix_order = matrix.shape[-1]
    factor = jnp.linalg.cholesky(matrix)
    identity = jnp.broadcast_to(jnp.eye(matrix_order, dtype=matrix.dtype), matrix.shape)
    lower_inv = lax.linalg.triangular_solve(factor, identity, left_side=True, lower=True)
    return jnp.einsum("...ka,...kb->...ab", lower_inv, lower_inv, precision=precise)


def prepare(normal_mat, coupling, lengths):
    stations = coupling.shape[0]
    block_len = coupling.shape[3]
    positions = jnp.arange(block_len, dtype=jnp.int32)
    row_valid = (positions[None, :] < lengths[:, None]).astype(jnp.float32)
    keep_mask = row_valid[:, :, None] * row_valid[:, None, :]
    stacked = normal_mat.reshape(stations, block_len, block_len)
    effective = keep_mask * stacked + (1.0 - keep_mask) * jnp.eye(block_len, dtype=jnp.float32)
    inverse = spd_inverse(effective)
    weighted = coupling * row_valid[:, None, None, :, None]
    solved = jnp.einsum("sab,shjbc->shjac", inverse, weighted, precision=precise)
    return (keep_mask, inverse, weighted, solved)


def finish_cov(keep_mask, inverse, bias_part, unimod):
    stations = keep_mask.shape[0]
    block_len = keep_mask.shape[1]
    covariance = keep_mask * (inverse + bias_part)
    integer_map = unimod.reshape(stations, block_len, block_len).astype(jnp.float32)
    mapped = jnp.einsum("sab,sbc,sdc->sad", integer_map, covariance, integer_map, precision=precise)
    return (keep_mask * mapped).reshape(stations, block_len * block_len)


def local(normal_mat, coupling, lengths, visible, bias_prior, unimod):
    keep_mask, inverse, weighted, solved = prepare(normal_mat, coupling, lengths)
    reduced = jnp.einsum("shjac,shjad->shjcd", weighted, weighted - solved, precision=precise)
    block_width = coupling.shape[4]
    identity = jnp.eye(block_width, dtype=jnp.float32)
    columns = jnp.arange(NHALF, dtype=jnp.int32)
    selector = (visible[..., None] == columns).astype(jnp.float32)
    block_table = jnp.einsum("shjx,shjcd->hxcd", selector, reduced, precision=precise)
    local_sum = lax.psum_scatter(block_table, "station", scatter_dimension=1, tiled=True)
    block_sum = lax.psum(local_sum, "group")
    bias_cov = spd_inverse(block_sum + bias_prior[..., :, None] * identity)
    segment = lax.all_gather(bias_cov, "station", axis=1, tiled=True)
    piece_len = segment.shape[1]
    local_pick = (visible[..., None] == jnp.arange(piece_len, dtype=jnp.int32)).astype(jnp.float32)
    chosen = jnp.einsum("shjx,hxcd->shjcd", local_pick, segment, precision=precise)
    lifted = jnp.einsum("shjac,shjcd->shjad", solved, chosen, precision=precise)
    bias_part = jnp.einsum("shjad,shjbd->sab", lifted, solved, precision=precise)
    combined = lax.psum(bias_part.reshape(bias_part.shape[0], -1), "bias")
    amb_cov = finish_cov(keep_mask, inverse, combined.reshape(bias_part.shape), unimod)
    return (bias_cov, amb_cov)


def solution(mesh):
    return jax.shard_map(
        local,
        mesh=mesh,
        in_specs=(
            P(("station", "group"), None),
            P(("station", "group"), "bias", None, None, None),
            P(("station", "group")),
            P(("station", "group"), "bias", None),
            P("bias", "station", None),
            P(("station", "group"), None),
        ),
        out_specs=(P("bias", "station", None, None), P(("station", "group"), None)),
        check_vma=False,
    )
```

profile of v0, /device:TPU:0, one launch (start us, length us, event | category | flops | bytes accessed | tf_op | source)
XLA Modules:
  0.0 314.8 jit_solution(5613608994066356341)
XLA Ops:
  7.3 0.7 fusion.43
  8.1 1.0 reshape.177
  9.2 0.1 fusion.24
  9.4 0.1 fusion.30
  9.6 35.2 %custom-call.14 = f32[8,48,48]{2,1,0:T(8,128)S(1)} custom-call(f32[8,48,48]{2,1,0:T(8,128)S(1)} %fusion.30), custom_call_target="Cholesky" | custom-call | tf_op jit(solution)/shard_map/jit(cholesky)/cholesky | solution.py:12
  45.0 29.5 %custom-call.15 = f32[8,1,48,48]{2,3,1,0:T(8,128)S(1)} custom-call(f32[8,1,48,48]{3,2,1,0:T(8,128)S(1)} %select_bitcast_fusion.1), custom_call_target="InvertDiagBlocksLowerTriangular" | custom-call | tf_op jit(solution)/shard_map/triangular_solve | solution.py:14
  74.6 0.5 fusion.28
  75.1 0.5 fusion.44
  75.6 1.7 fusion.10
  77.3 6.9 %fusion.7 = f32[8,8,128,128]{3,2,1,0:T(8,128)S(1)} fusion(f32[8,8,128,48]{2,3,1,0:T(8,128)S(1)} %fusion.10, f32[8,1,8,48,128]{4,3,2,1,0:T(8,128)S(1)} %copy-done, f32[8,48]{1,0:T(8,128)S(1)} %fusion.43), kind=kOutput, calls=%fused_computation.9 | convolution fusion | flops 605159424 | bytes 7341568 | tf_op jit(solution)/shard_map/shjac,shjad->shjcd/dot_general | solution.py:43
  84.2 4.1 %fusion.12 = f32[16,128,128]{2,0,1:T(8,128)S(1)} fusion(f32[8,8,128,128]{3,2,1,0:T(8,128)S(1)} %fusion.7, s32[8,8]{1,0:T(8,128)S(1)} %bitcast.86), kind=kOutput, calls=%fused_computation.14 | convolution fusion | flops 201327616 | bytes 5243136 | tf_op jit(solution)/shard_map/shjx,shjcd->hxcd/dot_general | solution.py:48
  88.3 1.4 copy.62
  89.9 30.1 %reduce-scatter.2.cloned.1.call-done = f32[1,4,128,128]{2,3,1,0:T(8,128)} async-done(((f32[1,16,128,128]{2,3,1,0:T(8,128)}), f32[1,4,128,128]{2,3,1,0:T(8,128)}) %reduce-scatter.2.cloned.1.call-update) | async-done | bytes 262160 | tf_op jit(solution)/shard_map/reduce_scatter | solution.py:49
  120.2 32.9 %all-reduce.3.cloned.1.call-done = f32[1,4,128,128]{2,3,1,0:T(8,128)} async-done(((f32[1,4,128,128]{2,3,1,0:T(8,128)}), f32[1,4,128,128]{2,3,1,0:T(8,128)}) %all-reduce.3.cloned.1.call-update) | async-done | bytes 262160 | tf_op jit(solution)/shard_map/psum | solution.py:50
  153.1 1.0 multiply_add_fusion
  154.1 0.1 copy.64
  154.2 1.0 fusion.23
  155.3 46.9 %custom-call.16 = f32[1,4,128,128]{3,2,1,0:T(8,128)S(1)} custom-call(f32[1,4,128,128]{3,2,1,0:T(8,128)S(1)} %fusion.23), custom_call_target="Cholesky" | custom-call | tf_op jit(solution)/shard_map/jit(cholesky)/cholesky | solution.py:12
  202.2 0.1 compare_reduce_fusion.1
  202.4 39.3 %custom-call.17 = f32[1,4,1,128,128]{3,4,2,1,0:T(8,128)S(1)} custom-call(f32[1,4,1,128,128]{4,3,2,1,0:T(8,128)S(1)} %select_bitcast_fusion), custom_call_target="InvertDiagBlocksLowerTriangular" | custom-call | tf_op jit(solution)/shard_map/triangular_solve | solution.py:14
  241.8 0.6 fusion.21
  242.3 1.3 fusion.45
  243.7 0.3 all-reduce.5.cloned.1.call-start
  243.9 27.9 %all-gather.3.cloned.1.call-done = f32[16,128,128]{2,1,0:T(8,128)} async-done(((f32[4,128,128]{2,1,0:T(8,128)}), f32[16,128,128]{2,1,0:T(8,128)}) %all-gather.3.cloned.1.call-update) | async-done | bytes 1048592 | tf_op jit(solution)/shard_map/all_gather | solution.py:52
  271.8 3.3 %convolution_bitcast_fusion = f32[8,8,128,128]{3,1,0,2:T(8,128)S(1)} fusion(f32[16,128,128,1]{2,1,0,3:T(8,128)} %bitcast.85, s32[8,8]{1,0:T(8,128)S(1)} %bitcast.87), kind=kOutput, calls=%fused_computation.4 | convolution fusion | flops 201327616 | bytes 5243136 | tf_op jit(solution)/shard_map/shjx,hxcd->shjcd/dot_general | solution.py:55
  275.1 6.0 %fusion = f32[8,8,48,128]{3,2,1,0:T(8,128)S(1)} fusion(f32[8,8,128,48]{2,3,1,0:T(8,128)S(1)} %fusion.10, f32[8,8,128,128]{3,1,0,2:T(8,128)S(1)} %convolution_bitcast_fusion), kind=kOutput, calls=%fused_computation | convolution fusion | flops 603979776 | bytes 7340032 | tf_op jit(solution)/shard_map/shjac,shjcd->shjad/dot_general | solution.py:56
  281.1 2.4 fusion.15
  283.7 0.1 convert_element_type.47
  283.8 21.7 %all-reduce.5.cloned.1.call-done = f32[8,48,48]{1,2,0:T(8,128)} async-done(((f32[8,48,48]{1,2,0:T(8,128)}), f32[8,48,48]{1,2,0:T(8,128)}) %all-reduce.5.cloned.1.call-update) | async-done | bytes 73744 | tf_op jit(solution)/shard_map/psum | solution.py:58
  305.5 1.4 fusion.26
  306.9 0.4 convolution_multiply_fusion
  307.5 0.8 reshape.185
  (33 shorter events, 1.3 us)
Async XLA Ops:
  7.2 112.8 %reduce-scatter.2.cloned.1.call-start = ((), (), s32[]{:S(2)}) async-start(), calls=%async_computation.1 | async-start | bytes 1310720 | tf_op jit(solution)/shard_map/reduce_scatter | solution.py:49
  9.2 66.4 %copy-start = (f32[8,1,8,48,128]{4,3,2,1,0:T(8,128)S(1)}, f32[8,1,8,48,128]{4,3,2,1,0:T(8,128)}, u32[]{:S(2)}) copy-start(f32[8,1,8,48,128]{4,3,2,1,0:T(8,128)} %param.7) | copy-start | bytes 4718596
  77.3 6.9 %copy-start.2 = (s32[8,1,8]{2,1,0:T(1,128)S(1)}, s32[8,1,8]{2,1,0:T(1,128)}, u32[]{:S(2)}) copy-start(s32[8,1,8]{2,1,0:T(1,128)} %param.9) | copy-start | bytes 772
  88.3 64.8 %copy-start.3 = (f32[1,4,128]{2,1,0:T(4,128)S(1)}, f32[1,4,128]{2,1,0:T(4,128)}, u32[]{:S(2)}) copy-start(f32[1,4,128]{2,1,0:T(4,128)} %param.10) | copy-start | bytes 6148
  89.8 63.3 %all-reduce.3.cloned.1.call-start = ((), (), s32[]{:S(2)}) async-start(), calls=%async_computation.2 | async-start | bytes 524288 | tf_op jit(solution)/shard_map/psum | solution.py:50
  120.0 151.8 %all-gather.3.cloned.1.call-start = ((), (), s32[]{:S(2)}) async-start(), calls=%async_computation.4 | async-start | bytes 1310720 | tf_op jit(solution)/shard_map/all_gather | solution.py:52
  243.7 61.8 %all-reduce.5.cloned.1.call-start = ((), (), s32[]{:S(2)}) async-start(), calls=%async_computation.3 | async-start | bytes 393216 | tf_op jit(solution)/shard_map/psum | solution.py:58
  281.1 2.5 copy-start.1
Sparse Core Ops, SparseCore 0:
  89.9 29.9 reduce-scatter.1
  122.3 30.7 all-reduce.2
  243.8 27.9 all-gather.2
  283.6 21.7 all-reduce.4
where the time goes:
time: 315 us
  other arithmetic  154 us (49%)
  waiting for transfers between devices  113 us (36%)
  matrix products  29.1 us (9%)
  between operations  14.1 us (4%)
  local copies, waits for them, and re-layouts  4.08 us (1%)
    another operation x8, other arithmetic, spd_inverse(): factor = jnp.linalg.cholesky(matrix)  82.4 us
    another operation x6, other arithmetic, spd_inverse(): lax.linalg.triangular_solve(factor, identity, left_side=True, lower=True)  69.1 us
    psum x1, waiting for transfers between devices, local(): block_sum = lax.psum(local_sum, 'group')  32.9 us
    reduce_scatter x1, waiting for transfers between devices, local(): lax.psum_scatter(block_table, 'station', scatter_dimension=1, tiled=True)  30.1 us
    all_gather x1, waiting for transfers between devices, local(): segment = lax.all_gather(bias_cov, 'station', axis=1, tiled=True)  27.9 us
    psum x1, waiting for transfers between devices, local(): combined = lax.psum(bias_part.reshape(bias_part.shape[0], -1), 'bias')  21.7 us
    dot_general x1, matrix products, local(): jnp.einsum('shjac,shjad->shjcd', weighted, weighted - solved, precision=p...  6.89 us
  transfers between devices with their start and end apart: 4, of which 4 were waited for; matrix products, arithmetic and copies ran while one was open for 0% of the time, Pallas kernels for 0%

commit v1 on v0

--- a/solution.py
+++ b/solution.py
@@ -5,6 +5,7 @@
 
 NHALF = 16
 precise = lax.Precision.HIGHEST
+roads_wait = lambda x_in: jnp.concatenate(jax.lax.all_gather(x_in, "station"), 1)
 
 
 def spd_inverse(matrix):
@@ -49,7 +50,7 @@
     local_sum = lax.psum_scatter(block_table, "station", scatter_dimension=1, tiled=True)
     block_sum = lax.psum(local_sum, "group")
     bias_cov = spd_inverse(block_sum + bias_prior[..., :, None] * identity)
-    segment = lax.all_gather(bias_cov, "station", axis=1, tiled=True)
+    segment = roads_wait(bias_cov)
     piece_len = segment.shape[1]
     local_pick = (visible[..., None] == jnp.arange(piece_len, dtype=jnp.int32)).astype(jnp.float32)
     chosen = jnp.einsum("shjx,hxcd->shjcd", local_pick, segment, precision=precise)

time: 315 us -> 315 us (level)
  no operation moved by 1% of the time
where the time goes in v1:
time: 315 us
  other arithmetic  154 us (49%)
  waiting for transfers between devices  113 us (36%)
  matrix products  29.1 us (9%)
  between operations  14.1 us (4%)
  local copies, waits for them, and re-layouts  4.08 us (1%)
    another operation x8, other arithmetic, spd_inverse(): factor = jnp.linalg.cholesky(matrix)  82.4 us
    another operation x6, other arithmetic, spd_inverse(): lax.linalg.triangular_solve(factor, identity, left_side=True, lower=True)  69.1 us
    psum x1, waiting for transfers between devices, local(): block_sum = lax.psum(local_sum, 'group')  32.9 us
    reduce_scatter x1, waiting for transfers between devices, local(): lax.psum_scatter(block_table, 'station', scatter_dimension=1, tiled=True)  30.1 us
    all_gather x1, waiting for transfers between devices, jax.lax.all_gather(x_in, 'station')  27.9 us
    psum x1, waiting for transfers between devices, local(): combined = lax.psum(bias_part.reshape(bias_part.shape[0], -1), 'bias')  21.7 us
    dot_general x1, matrix products, local(): jnp.einsum('shjac,shjad->shjcd', weighted, weighted - solved, precision=p...  6.89 us
  transfers between devices with their start and end apart: 4, of which 4 were waited for; matrix products, arithmetic and copies ran while one was open for 0% of the time, Pallas kernels for 0%

profile of v1, /device:TPU:0, one launch (start us, length us, event | category | flops | bytes accessed | tf_op | source)
XLA Modules:
  0.0 314.8 jit_solution(5613608994066356341)
XLA Ops:
  7.3 0.7 fusion.43
  8.1 1.0 reshape.180
  9.2 0.1 fusion.24
  9.4 0.1 fusion.30
  9.6 35.2 %custom-call.14 = f32[8,48,48]{2,1,0:T(8,128)S(1)} custom-call(f32[8,48,48]{2,1,0:T(8,128)S(1)} %fusion.30), custom_call_target="Cholesky" | custom-call | tf_op jit(solution)/shard_map/jit(cholesky)/cholesky | solution.py:13
  45.0 29.5 %custom-call.15 = f32[8,1,48,48]{2,3,1,0:T(8,128)S(1)} custom-call(f32[8,1,48,48]{3,2,1,0:T(8,128)S(1)} %select_bitcast_fusion.1), custom_call_target="InvertDiagBlocksLowerTriangular" | custom-call | tf_op jit(solution)/shard_map/triangular_solve | solution.py:15
  74.6 0.5 fusion.28
  75.1 0.5 fusion.44
  75.6 1.7 fusion.10
  77.3 6.9 %fusion.7 = f32[8,8,128,128]{3,2,1,0:T(8,128)S(1)} fusion(f32[8,8,128,48]{2,3,1,0:T(8,128)S(1)} %fusion.10, f32[8,1,8,48,128]{4,3,2,1,0:T(8,128)S(1)} %copy-done, f32[8,48]{1,0:T(8,128)S(1)} %fusion.43), kind=kOutput, calls=%fused_computation.9 | convolution fusion | flops 605159424 | bytes 7341568 | tf_op jit(solution)/shard_map/shjac,shjad->shjcd/dot_general | solution.py:44
  84.2 4.1 %fusion.12 = f32[16,128,128]{2,0,1:T(8,128)S(1)} fusion(f32[8,8,128,128]{3,2,1,0:T(8,128)S(1)} %fusion.7, s32[8,8]{1,0:T(8,128)S(1)} %bitcast.86), kind=kOutput, calls=%fused_computation.14 | convolution fusion | flops 201327616 | bytes 5243136 | tf_op jit(solution)/shard_map/shjx,shjcd->hxcd/dot_general | solution.py:49
  88.3 1.4 copy.62
  89.9 30.1 %reduce-scatter.2.cloned.1.call-done = f32[1,4,128,128]{2,3,1,0:T(8,128)} async-done(((f32[1,16,128,128]{2,3,1,0:T(8,128)}), f32[1,4,128,128]{2,3,1,0:T(8,128)}) %reduce-scatter.2.cloned.1.call-update) | async-done | bytes 262160 | tf_op jit(solution)/shard_map/reduce_scatter | solution.py:50
  120.2 32.9 %all-reduce.3.cloned.1.call-done = f32[1,4,128,128]{2,3,1,0:T(8,128)} async-done(((f32[1,4,128,128]{2,3,1,0:T(8,128)}), f32[1,4,128,128]{2,3,1,0:T(8,128)}) %all-reduce.3.cloned.1.call-update) | async-done | bytes 262160 | tf_op jit(solution)/shard_map/psum | solution.py:51
  153.1 1.0 multiply_add_fusion
  154.1 0.1 copy.64
  154.2 1.0 fusion.23
  155.3 46.9 %custom-call.16 = f32[1,4,128,128]{3,2,1,0:T(8,128)S(1)} custom-call(f32[1,4,128,128]{3,2,1,0:T(8,128)S(1)} %fusion.23), custom_call_target="Cholesky" | custom-call | tf_op jit(solution)/shard_map/jit(cholesky)/cholesky | solution.py:13
  202.2 0.1 compare_reduce_fusion.1
  202.4 39.3 %custom-call.17 = f32[1,4,1,128,128]{3,4,2,1,0:T(8,128)S(1)} custom-call(f32[1,4,1,128,128]{4,3,2,1,0:T(8,128)S(1)} %select_bitcast_fusion), custom_call_target="InvertDiagBlocksLowerTriangular" | custom-call | tf_op jit(solution)/shard_map/triangular_solve | solution.py:15
  241.8 0.6 fusion.21
  242.3 1.3 fusion.45
  243.7 0.3 all-reduce.5.cloned.1.call-start
  243.9 27.9 %all-gather.3.cloned.1.call-done = f32[16,128,128]{2,1,0:T(8,128)} async-done(((f32[4,128,128]{2,1,0:T(8,128)}), f32[16,128,128]{2,1,0:T(8,128)}) %all-gather.3.cloned.1.call-update) | async-done | bytes 1048592 | tf_op jit(solution)/shard_map/all_gather | solution.py:8
  271.8 3.3 %convolution_bitcast_fusion = f32[8,8,128,128]{3,1,0,2:T(8,128)S(1)} fusion(f32[16,128,128,1]{2,1,0,3:T(8,128)} %bitcast.85, s32[8,8]{1,0:T(8,128)S(1)} %bitcast.87), kind=kOutput, calls=%fused_computation.4 | convolution fusion | flops 201327616 | bytes 5243136 | tf_op jit(solution)/shard_map/shjx,hxcd->shjcd/dot_general | solution.py:56
  275.1 6.0 %fusion = f32[8,8,48,128]{3,2,1,0:T(8,128)S(1)} fusion(f32[8,8,128,48]{2,3,1,0:T(8,128)S(1)} %fusion.10, f32[8,8,128,128]{3,1,0,2:T(8,128)S(1)} %convolution_bitcast_fusion), kind=kOutput, calls=%fused_computation | convolution fusion | flops 603979776 | bytes 7340032 | tf_op jit(solution)/shard_map/shjac,shjcd->shjad/dot_general | solution.py:57
  281.1 2.4 fusion.15
  283.7 0.1 convert_element_type.47
  283.8 21.7 %all-reduce.5.cloned.1.call-done = f32[8,48,48]{1,2,0:T(8,128)} async-done(((f32[8,48,48]{1,2,0:T(8,128)}), f32[8,48,48]{1,2,0:T(8,128)}) %all-reduce.5.cloned.1.call-update) | async-done | bytes 73744 | tf_op jit(solution)/shard_map/psum | solution.py:59
  305.5 1.4 fusion.26
  306.9 0.4 convolution_multiply_fusion
  307.5 0.8 reshape.188
  (33 shorter events, 1.3 us)
Async XLA Ops:
  7.2 112.8 %reduce-scatter.2.cloned.1.call-start = ((), (), s32[]{:S(2)}) async-start(), calls=%async_computation.1 | async-start | bytes 1310720 | tf_op jit(solution)/shard_map/reduce_scatter | solution.py:50
  9.2 66.4 %copy-start = (f32[8,1,8,48,128]{4,3,2,1,0:T(8,128)S(1)}, f32[8,1,8,48,128]{4,3,2,1,0:T(8,128)}, u32[]{:S(2)}) copy-start(f32[8,1,8,48,128]{4,3,2,1,0:T(8,128)} %param.7) | copy-start | bytes 4718596
  77.3 6.9 %copy-start.2 = (s32[8,1,8]{2,1,0:T(1,128)S(1)}, s32[8,1,8]{2,1,0:T(1,128)}, u32[]{:S(2)}) copy-start(s32[8,1,8]{2,1,0:T(1,128)} %param.9) | copy-start | bytes 772
  88.3 64.8 %copy-start.3 = (f32[1,4,128]{2,1,0:T(4,128)S(1)}, f32[1,4,128]{2,1,0:T(4,128)}, u32[]{:S(2)}) copy-start(f32[1,4,128]{2,1,0:T(4,128)} %param.10) | copy-start | bytes 6148
  89.8 63.3 %all-reduce.3.cloned.1.call-start = ((), (), s32[]{:S(2)}) async-start(), calls=%async_computation.2 | async-start | bytes 524288 | tf_op jit(solution)/shard_map/psum | solution.py:51
  120.0 151.8 %all-gather.3.cloned.1.call-start = ((), (), s32[]{:S(2)}) async-start(), calls=%async_computation.4 | async-start | bytes 1310720 | tf_op jit(solution)/shard_map/all_gather | solution.py:8
  243.7 61.8 %all-reduce.5.cloned.1.call-start = ((), (), s32[]{:S(2)}) async-start(), calls=%async_computation.3 | async-start | bytes 393216 | tf_op jit(solution)/shard_map/psum | solution.py:59
  281.1 2.5 copy-start.1
Sparse Core Ops, SparseCore 0:
  89.9 29.9 reduce-scatter.1
  122.3 30.7 all-reduce.2
  243.8 27.9 all-gather.2
  283.6 21.7 all-reduce.4
